TPU v7x, 128 devices: a whole 4x4x4 slice. The times are simulated.
128 devices in a mesh: seq: 32 (over x, y, core), tp: 4 (over z).
Axes of the slice: x: 4, y: 4, z: 4, core: 2. Of those that a mesh axis runs over, the one named last changes fastest.
Arguments:
- states_in: bfloat16 [8192, 2048], P('seq'), may hold values from -7 to 7
- lengths: int32 [4], replicated, may hold values from 1 to 64, 128 in all
- attn_gain: float32 [2048], replicated, may hold values from 0.5 to 1.5
- w_query: bfloat16 [2048, 2048], P(None, 'tp'), may hold values from -0.125 to 0.125
- w_key: bfloat16 [2048, 2048], P(None, 'tp'), may hold values from -0.088388348 to 0.088388348
- w_value: bfloat16 [2048, 4096], P(None, 'tp'), may hold values from -0.125 to 0.125
- w_gate: bfloat16 [2048, 4096], P(None, 'tp'), may hold values from -0.125 to 0.125
- w_beta: bfloat16 [2048, 16], P(None, 'tp'), may hold values from -1 to 1
- w_alpha: bfloat16 [2048, 16], P(None, 'tp'), may hold values from -0.125 to 0.125
- decay_rate: float32 [16], P('tp'), may hold values from 4.8828125e-05 to 0.05
- decay_bias: float32 [16], P('tp'), may hold values from -2 to 1
- conv_query: float32 [4, 2048], P(None, 'tp'), may hold values from -3 to 3
- conv_key: float32 [4, 2048], P(None, 'tp'), may hold values from -3 to 3
- conv_value: float32 [4, 4096], P(None, 'tp'), may hold values from -4.5 to 4.5
- out_gain: float32 [256], replicated, may hold values from 0.5 to 1.5
- w_out: bfloat16 [4096, 2048], P('tp'), may hold values from -0.09375 to 0.09375
- final_gain: float32 [2048], replicated, may hold values from 0.5 to 1.5
- w_head: bfloat16 [2048, 32000], P(None, ('seq', 'tp')), may hold values from -0.41992188 to 0.41992188
Outputs:
- hidden: bfloat16 [8192, 2048], P('seq', 'tp')
- block_states: float32 [128, 16, 128, 256], P('seq', 'tp')
- max_logit: float32 [4], replicated
Inputs may be any that keep to these rules, and one draw needn't show every extreme that they name: Prompt lengths are counted in blocks of 64 tokens; they sum to 128 and the longest is 64.
All inputs are finite; a program needn't handle non-finite values.
Results may differ from a plain program's by a relative error of at most 0.0095.
Values may be sent and summed in bfloat16 or wider, within the bound.
No kernel may reach another device: no remote copies, remote signals or barrier semaphores. Data moves between devices by JAX's collectives and lax.ppermute only.
A program may use at most 128 MiB of HBM per device.

v0:
```python
import jax
import jax.numpy as jnp
from jax import lax
from jax.sharding import PartitionSpec as P

CONV = 4
BLOCK_LEN = 64
EPS = 1e-06
HIGH = lax.Precision.HIGHEST


def from_behind(value, axis, steps):
    count = lax.axis_size(axis)
    first, last = (max(0, -steps), min(count, count - steps))
    return lax.ppermute(value, axis, [(source, source + steps) for source in range(first, last)])


def rms_scale(values, gain):
    return values * lax.rsqrt(jnp.mean(values * values, axis=-1, keepdims=True) + EPS) * gain


def unit_rows(values):
    return values * lax.rsqrt(jnp.sum(values * values, axis=-1, keepdims=True) + EPS)


def request_start(positions, offsets, block_len):
    block_ids = positions // block_len
    hits = offsets[None, :] <= block_ids[:, None]
    return block_len * jnp.max(jnp.where(hits, offsets[None, :], 0), axis=1)


def short_conv(extended, positions, start_tok, weight):
    row_count = positions.shape[0]
    tap_count = weight.shape[0]
    running = jnp.zeros((row_count, extended.shape[1]), jnp.float32)
    for tap_index in range(tap_count):
        lag_steps = tap_count - 1 - tap_index
        shifted = extended[tap_index : tap_index + row_count].astype(jnp.float32)
        valid = (positions - lag_steps >= start_tok)[:, None]
        running = running + jnp.where(valid, shifted, 0.0) * weight[tap_index]
    return jax.nn.silu(running)


def block_step(carry_state, block_inputs):
    q_rows, k_rows, v_rows, beta_rows, log_cum, keep_flag = block_inputs
    carry_state = carry_state * keep_flag
    block_len = q_rows.shape[1]
    row_ids = lax.broadcasted_iota(jnp.int32, (block_len, block_len), 0)
    col_ids = lax.broadcasted_iota(jnp.int32, (block_len, block_len), 1)
    on_lower = (row_ids >= col_ids).astype(jnp.float32)
    off_lower = (row_ids > col_ids).astype(jnp.float32)
    log_gap = log_cum[:, :, None] - log_cum[:, None, :]
    decays = jnp.exp(jnp.where(row_ids >= col_ids, log_gap, 0.0)) * on_lower
    growth = jnp.exp(log_cum)
    key_gram = jnp.einsum("hid,hjd->hij", k_rows, k_rows, precision=HIGH)
    system_mat = (
        jnp.eye(block_len, dtype=jnp.float32)
        + beta_rows[:, :, None] * key_gram * decays * off_lower
    )
    carried = jnp.einsum("hid,hde->hie", k_rows, carry_state, precision=HIGH)
    right_side = beta_rows[:, :, None] * (v_rows - growth[:, :, None] * carried)
    pseudo_values = lax.linalg.triangular_solve(
        system_mat, right_side, left_side=True, lower=True, unit_diagonal=True
    )
    scores = jnp.einsum("hid,hjd->hij", q_rows, k_rows, precision=HIGH) * decays
    output = growth[:, :, None] * jnp.einsum("hid,hde->hie", q_rows, carry_state, precision=HIGH)
    output = output + jnp.einsum("hij,hje->hie", scores, pseudo_values, precision=HIGH)
    tail_decay = jnp.exp(log_cum[:, -1:] - log_cum)
    carry_state = jnp.exp(log_cum[:, -1])[:, None, None] * carry_state + jnp.einsum(
        "hjd,hje->hde", k_rows * tail_decay[:, :, None], pseudo_values, precision=HIGH
    )
    return (carry_state, (output, carry_state))


def to_blocks(values, block_count, head_count):
    return values.reshape(block_count, BLOCK_LEN, head_count, -1).transpose(0, 2, 1, 3)


def body(
    states_in,
    lengths,
    attn_gain,
    w_query,
    w_key,
    w_value,
    w_gate,
    w_beta,
    w_alpha,
    decay_rate,
    decay_bias,
    conv_query,
    conv_key,
    conv_value,
    out_gain,
    w_out,
    final_gain,
    w_head,
):
    tok_dev = states_in.shape[0]
    heads_dev = decay_rate.shape[0]
    key_dim = w_query.shape[1] // heads_dev
    value_dim = w_value.shape[1] // heads_dev
    blocks_dev = tok_dev // BLOCK_LEN
    piece_index = lax.axis_index("seq")
    x_float = states_in.astype(jnp.float32)
    normed = rms_scale(x_float, attn_gain).astype(jnp.bfloat16)
    pre_q = jnp.dot(normed, w_query, preferred_element_type=jnp.float32).astype(jnp.bfloat16)
    pre_k = jnp.dot(normed, w_key, preferred_element_type=jnp.float32).astype(jnp.bfloat16)
    pre_v = jnp.dot(normed, w_value, preferred_element_type=jnp.float32).astype(jnp.bfloat16)
    gate_raw = jnp.dot(normed, w_gate, preferred_element_type=jnp.float32)
    beta_all = jax.nn.sigmoid(jnp.dot(normed, w_beta, preferred_element_type=jnp.float32))
    log_decay = -decay_rate * jax.nn.softplus(
        jnp.dot(normed, w_alpha, preferred_element_type=jnp.float32) + decay_bias
    )
    ends = jnp.cumsum(lengths)
    offsets = ends - lengths
    positions = piece_index * tok_dev + jnp.arange(tok_dev, dtype=jnp.int32)
    start_tok = request_start(positions, offsets, BLOCK_LEN)
    local_pre = jnp.concatenate([pre_q, pre_k, pre_v], axis=1)
    prev_edge = from_behind(local_pre[tok_dev - (CONV - 1) :], "seq", 1)
    extended = jnp.concatenate([prev_edge, local_pre], axis=0)
    conv_weights = jnp.concatenate([conv_query, conv_key, conv_value], axis=1)
    conv_all = short_conv(extended, positions, start_tok, conv_weights)
    qk_width = heads_dev * key_dim
    q_heads = unit_rows(conv_all[:, :qk_width].reshape(tok_dev, heads_dev, key_dim)) * key_dim ** (
        -0.5
    )
    k_heads = unit_rows(conv_all[:, qk_width : 2 * qk_width].reshape(tok_dev, heads_dev, key_dim))
    q_blocks = to_blocks(q_heads, blocks_dev, heads_dev)
    k_blocks = to_blocks(k_heads, blocks_dev, heads_dev)
    v_blocks = to_blocks(conv_all[:, 2 * qk_width :], blocks_dev, heads_dev)
    v_augmented = jnp.concatenate(
        [jnp.zeros(v_blocks.shape[:3] + (key_dim,), jnp.float32), v_blocks], axis=3
    )
    beta_blocks = beta_all.reshape(blocks_dev, BLOCK_LEN, heads_dev).transpose(0, 2, 1)
    log_blocks = jnp.cumsum(
        log_decay.reshape(blocks_dev, BLOCK_LEN, heads_dev).transpose(0, 2, 1), axis=2
    )
    block_ids = piece_index * blocks_dev + jnp.arange(blocks_dev, dtype=jnp.int32)
    keep_flags = 1.0 - jnp.max((offsets[None, :] == block_ids[:, None]).astype(jnp.float32), axis=1)
    eye_heads = jnp.broadcast_to(jnp.eye(key_dim, dtype=jnp.float32), (heads_dev, key_dim, key_dim))
    initial = jnp.concatenate(
        [eye_heads, jnp.zeros((heads_dev, key_dim, value_dim), jnp.float32)], axis=2
    )
    final_aug, (out_aug, states_aug) = lax.scan(
        block_step, initial, (q_blocks, k_blocks, v_augmented, beta_blocks, log_blocks, keep_flags)
    )
    lin_map = final_aug[:, :, :key_dim]
    offset_state = final_aug[:, :, key_dim:]

    def relay_turn(turn_index, incoming):
        outgoing = jnp.einsum("hde,hef->hdf", lin_map, incoming, precision=HIGH) + offset_state
        return from_behind(outgoing, "seq", 1)

    incoming = lax.fori_loop(0, lax.axis_size("seq") - 1, relay_turn, jnp.zeros_like(offset_state))
    o_blocks = out_aug[..., key_dim:] + jnp.einsum(
        "bhcd,hde->bhce", out_aug[..., :key_dim], incoming, precision=HIGH
    )
    block_states = (
        jnp.einsum("bhde,hef->bhdf", states_aug[..., :key_dim], incoming, precision=HIGH)
        + states_aug[..., key_dim:]
    )
    o_tokens = o_blocks.transpose(0, 2, 1, 3).reshape(tok_dev, heads_dev, value_dim)
    gated = (
        rms_scale(o_tokens, out_gain) * jax.nn.silu(gate_raw.reshape(tok_dev, heads_dev, value_dim))
    ).astype(jnp.bfloat16)
    partial_out = jnp.dot(
        gated.reshape(tok_dev, heads_dev * value_dim), w_out, preferred_element_type=jnp.float32
    )
    model_width = x_float.shape[1]
    share_cols = model_width // lax.axis_size("tp")
    col_start = lax.axis_index("tp") * share_cols
    last_tok = ends * BLOCK_LEN - 1
    picker = (last_tok[:, None] == positions[None, :]).astype(jnp.bfloat16)
    summed = lax.psum(partial_out, "tp")
    hidden_full = (x_float + summed).astype(jnp.bfloat16)
    hidden = lax.dynamic_slice_in_dim(hidden_full, col_start, share_cols, 1)
    picked = jnp.dot(picker, hidden_full, preferred_element_type=jnp.float32)
    last_rows = lax.psum(picked.astype(jnp.bfloat16), "seq").astype(jnp.float32)
    final = rms_scale(last_rows, final_gain).astype(jnp.bfloat16)
    logits = jnp.dot(final, w_head, preferred_element_type=jnp.float32)
    max_logit = lax.pmax(jnp.max(logits, axis=1), ("seq", "tp"))
    return (hidden, block_states, max_logit)


def solution(mesh):
    return jax.shard_map(
        body,
        mesh=mesh,
        in_specs=(
            P("seq", None),
            P(),
            P(),
            P(None, "tp"),
            P(None, "tp"),
            P(None, "tp"),
            P(None, "tp"),
            P(None, "tp"),
            P(None, "tp"),
            P("tp"),
            P("tp"),
            P(None, "tp"),
            P(None, "tp"),
            P(None, "tp"),
            P(),
            P("tp", None),
            P(),
            P(None, ("seq", "tp")),
        ),
        out_specs=(P("seq", "tp"), P("seq", "tp", None, None), P()),
        check_vma=False,
    )
```

profile of v0, /device:TPU:1, one launch (start us, length us, event | category | flops | bytes accessed | tf_op | source)
XLA Modules:
  0.0 931.8 jit_solution(14299696759197903953)
XLA Ops:
  51.5 133.2 %while.24 = (s32[]{:T(128)}, f32[4,128,384]{2,1,0:T(8,128)S(1)}, f32[4,4,64,384]{3,2,0,1:T(8,128)}, f32[4,4,128,384]{3,2,1,0:T(8,128)}, f32[4,4,64]{2,1,0:T(4,12...) while((s32[]{:T(128)}, f32[4,128,384]{2,1,0:T(8,128)S(1)}, ...), condition=%wide.region_8.9_spmd, body=%wide.region_7.8_spmd.sunk | while | flops 656073024 | bytes 11045709 | solution.py:145
  54.5 20.4 %custom-call.8 = f32[4,1,64,64]{2,3,1,0:T(8,128)S(1)} custom-call(f32[4,1,64,64]{3,2,1,0:T(8,128)} %fusion.136), custom_call_target="InvertDiagBlocksLowerTriangular" | custom-call | tf_op jit(solution)/shard_map/while/body/eval_jaxpr/triangular_solve | solution.py:62
  87.8 20.4 %custom-call.8 = f32[4,1,64,64]{2,3,1,0:T(8,128)S(1)} custom-call(f32[4,1,64,64]{3,2,1,0:T(8,128)} %fusion.136), custom_call_target="InvertDiagBlocksLowerTriangular" | custom-call | tf_op jit(solution)/shard_map/while/body/eval_jaxpr/triangular_solve | solution.py:62
  121.1 20.4 %custom-call.8 = f32[4,1,64,64]{2,3,1,0:T(8,128)S(1)} custom-call(f32[4,1,64,64]{3,2,1,0:T(8,128)} %fusion.136), custom_call_target="InvertDiagBlocksLowerTriangular" | custom-call | tf_op jit(solution)/shard_map/while/body/eval_jaxpr/triangular_solve | solution.py:62
  154.4 20.4 %custom-call.8 = f32[4,1,64,64]{2,3,1,0:T(8,128)S(1)} custom-call(f32[4,1,64,64]{3,2,1,0:T(8,128)} %fusion.136), custom_call_target="InvertDiagBlocksLowerTriangular" | custom-call | tf_op jit(solution)/shard_map/while/body/eval_jaxpr/triangular_solve | solution.py:62
  185.6 428.0 %while.25 = (s32[]{:T(128)}, f32[4,128,256]{2,1,0:T(8,128)S(1)}, f32[4,128,128]{2,1,0:T(8,128)}, f32[4,128,256]{2,1,0:T(8,128)S(1)}, s32[]{:T(128)}) while((s32[]{:T(128)}, f32[4,128,256]{2,1,0:T(8,128)S(1)}, f32[4,128,128]{2,1,0:T(8,128)}, f32[4,128,256]{2,1,0:T(8,128)S(1)}, s32[]{:T(128)}) %tuple.75), condition=%wide.region_10.11_spmd, body=%wide.region_9.10_spmd.sunk | while | flops 201457664 | bytes 3932261 | solution.py:155
  215.9 6.4 collective-permute-done
  241.9 6.4 collective-permute-done
  268.0 6.4 collective-permute-done
  294.0 6.4 collective-permute-done
  307.1 6.4 collective-permute-done
  346.1 6.4 collective-permute-done
  372.2 6.4 collective-permute-done
  398.2 6.4 collective-permute-done
  440.7 6.4 collective-permute-done
  471.0 6.4 collective-permute-done
  516.4 6.4 collective-permute-done
  546.7 6.4 collective-permute-done
  576.9 6.4 collective-permute-done
  592.1 6.4 collective-permute-done
  620.6 8.3 fusion.47
  637.6 89.2 %all-reduce.4.cloned.1.call-done = f32[256,2048]{1,0:T(8,128)} async-done(((f32[256,2048]{1,0:T(8,128)}), f32[256,2048]{1,0:T(8,128)}) %all-reduce.4.cloned.1.call-update) | async-done | bytes 2097168 | tf_op jit(solution)/shard_map/psum | solution.py:175
  729.2 123.1 %psum.15 = bf16[4,2048]{1,0:T(4,128)(2,1)S(1)} all-reduce(bf16[4,2048]{1,0:T(4,128)(2,1)S(1)} %convolution_convert_fusion), channel_id=1, replica_groups=mesh['seq'=32,'tp'=4] {'seq'}, use_global_device_ids=true, to_apply=%region_13.14 | all-reduce | flops 8192 | bytes 32768 | tf_op jit(solution)/shard_map/psum | solution.py:179
  857.0 67.2 %pmax.7 = f32[4]{0:T(128)} all-reduce(f32[4]{0:T(128)S(1)} %convolution_reduce_fusion), channel_id=1, replica_groups=mesh['seq'=32,'tp'=4] {'seq','tp'}, use_global_device_ids=true, to_apply=%region_16.17 | all-reduce | flops 4 | bytes 32 | tf_op jit(solution)/shard_map/pmax | solution.py:182
  (303 shorter events, 457.3 us)
Async XLA Ops:
  7.2 719.6 %all-reduce.4.cloned.1.call-start = ((), (), s32[]{:S(2)}) async-start(), calls=%async_computation | async-start | bytes 4194304 | tf_op jit(solution)/shard_map/psum | solution.py:175
  15.9 12.0 %collective-permute-start.1 = (bf16[3,2048]{1,0:T(4,128)(2,1)S(1)}, bf16[3,2048]{1,0:T(4,128)(2,1)S(1)}, u32[]{:S(2)}, u32[]{:S(2)}) collective-permute-start(bf16[3,2048]{1,0:T(4,128)(2,1)S(1)} %slice.76), channel_id=1, source_target_pairs={{0,4},{4,8},{8,12},{12,16},{16,20},{20,24},{24,28},{28,32},{32,36}... | collective-permute-start | bytes 36872 | tf_op jit(solution)/shard_map/ppermute | solution.py:15
  211.6 10.7 %collective-permute-start = (f32[4,128,256]{2,1,0:T(8,128)}, f32[4,128,256]{2,1,0:T(8,128)S(1)}, u32[]{:S(2)}, u32[]{:S(2)}) collective-permute-start(f32[4,128,256]{2,1,0:T(8,128)} %convolution_add_fusion.5), channel_id=1, source_target_pairs={{0,4},{4,8},{8,12},{12,16},{16,20},{20,24},{24,28},{28,32},{32,36}... | collective-permute-start | bytes 1572872 | tf_op jit(solution)/shard_map/while/body/eval_jaxpr/ppermute | solution.py:15
  224.6 10.7 %collective-permute-start = (f32[4,128,256]{2,1,0:T(8,128)}, f32[4,128,256]{2,1,0:T(8,128)S(1)}, u32[]{:S(2)}, u32[]{:S(2)}) collective-permute-start(f32[4,128,256]{2,1,0:T(8,128)} %convolution_add_fusion.5), channel_id=1, source_target_pairs={{0,4},{4,8},{8,12},{12,16},{16,20},{20,24},{24,28},{28,32},{32,36}... | collective-permute-start | bytes 1572872 | tf_op jit(solution)/shard_map/while/body/eval_jaxpr/ppermute | solution.py:15
  250.7 10.7 %collective-permute-start = (f32[4,128,256]{2,1,0:T(8,128)}, f32[4,128,256]{2,1,0:T(8,128)S(1)}, u32[]{:S(2)}, u32[]{:S(2)}) collective-permute-start(f32[4,128,256]{2,1,0:T(8,128)} %convolution_add_fusion.5), channel_id=1, source_target_pairs={{0,4},{4,8},{8,12},{12,16},{16,20},{20,24},{24,28},{28,32},{32,36}... | collective-permute-start | bytes 1572872 | tf_op jit(solution)/shard_map/while/body/eval_jaxpr/ppermute | solution.py:15
  263.7 10.7 %collective-permute-start = (f32[4,128,256]{2,1,0:T(8,128)}, f32[4,128,256]{2,1,0:T(8,128)S(1)}, u32[]{:S(2)}, u32[]{:S(2)}) collective-permute-start(f32[4,128,256]{2,1,0:T(8,128)} %convolution_add_fusion.5), channel_id=1, source_target_pairs={{0,4},{4,8},{8,12},{12,16},{16,20},{20,24},{24,28},{28,32},{32,36}... | collective-permute-start | bytes 1572872 | tf_op jit(solution)/shard_map/while/body/eval_jaxpr/ppermute | solution.py:15
  276.7 10.7 %collective-permute-start = (f32[4,128,256]{2,1,0:T(8,128)}, f32[4,128,256]{2,1,0:T(8,128)S(1)}, u32[]{:S(2)}, u32[]{:S(2)}) collective-permute-start(f32[4,128,256]{2,1,0:T(8,128)} %convolution_add_fusion.5), channel_id=1, source_target_pairs={{0,4},{4,8},{8,12},{12,16},{16,20},{20,24},{24,28},{28,32},{32,36}... | collective-permute-start | bytes 1572872 | tf_op jit(solution)/shard_map/while/body/eval_jaxpr/ppermute | solution.py:15
  289.8 10.7 %collective-permute-start = (f32[4,128,256]{2,1,0:T(8,128)}, f32[4,128,256]{2,1,0:T(8,128)S(1)}, u32[]{:S(2)}, u32[]{:S(2)}) collective-permute-start(f32[4,128,256]{2,1,0:T(8,128)} %convolution_add_fusion.5), channel_id=1, source_target_pairs={{0,4},{4,8},{8,12},{12,16},{16,20},{20,24},{24,28},{28,32},{32,36}... | collective-permute-start | bytes 1572872 | tf_op jit(solution)/shard_map/while/body/eval_jaxpr/ppermute | solution.py:15
  315.8 10.7 %collective-permute-start = (f32[4,128,256]{2,1,0:T(8,128)}, f32[4,128,256]{2,1,0:T(8,128)S(1)}, u32[]{:S(2)}, u32[]{:S(2)}) collective-permute-start(f32[4,128,256]{2,1,0:T(8,128)} %convolution_add_fusion.5), channel_id=1, source_target_pairs={{0,4},{4,8},{8,12},{12,16},{16,20},{20,24},{24,28},{28,32},{32,36}... | collective-permute-start | bytes 1572872 | tf_op jit(solution)/shard_map/while/body/eval_jaxpr/ppermute | solution.py:15
  341.9 10.7 %collective-permute-start = (f32[4,128,256]{2,1,0:T(8,128)}, f32[4,128,256]{2,1,0:T(8,128)S(1)}, u32[]{:S(2)}, u32[]{:S(2)}) collective-permute-start(f32[4,128,256]{2,1,0:T(8,128)} %convolution_add_fusion.5), channel_id=1, source_target_pairs={{0,4},{4,8},{8,12},{12,16},{16,20},{20,24},{24,28},{28,32},{32,36}... | collective-permute-start | bytes 1572872 | tf_op jit(solution)/shard_map/while/body/eval_jaxpr/ppermute | solution.py:15
  354.9 10.7 %collective-permute-start = (f32[4,128,256]{2,1,0:T(8,128)}, f32[4,128,256]{2,1,0:T(8,128)S(1)}, u32[]{:S(2)}, u32[]{:S(2)}) collective-permute-start(f32[4,128,256]{2,1,0:T(8,128)} %convolution_add_fusion.5), channel_id=1, source_target_pairs={{0,4},{4,8},{8,12},{12,16},{16,20},{20,24},{24,28},{28,32},{32,36}... | collective-permute-start | bytes 1572872 | tf_op jit(solution)/shard_map/while/body/eval_jaxpr/ppermute | solution.py:15
  420.0 12.0 %collective-permute-start = (f32[4,128,256]{2,1,0:T(8,128)}, f32[4,128,256]{2,1,0:T(8,128)S(1)}, u32[]{:S(2)}, u32[]{:S(2)}) collective-permute-start(f32[4,128,256]{2,1,0:T(8,128)} %convolution_add_fusion.5), channel_id=1, source_target_pairs={{0,4},{4,8},{8,12},{12,16},{16,20},{20,24},{24,28},{28,32},{32,36}... | collective-permute-start | bytes 1572872 | tf_op jit(solution)/shard_map/while/body/eval_jaxpr/ppermute | solution.py:15
  434.4 12.8 %collective-permute-start = (f32[4,128,256]{2,1,0:T(8,128)}, f32[4,128,256]{2,1,0:T(8,128)S(1)}, u32[]{:S(2)}, u32[]{:S(2)}) collective-permute-start(f32[4,128,256]{2,1,0:T(8,128)} %convolution_add_fusion.5), channel_id=1, source_target_pairs={{0,4},{4,8},{8,12},{12,16},{16,20},{20,24},{24,28},{28,32},{32,36}... | collective-permute-start | bytes 1572872 | tf_op jit(solution)/shard_map/while/body/eval_jaxpr/ppermute | solution.py:15
  449.5 12.8 %collective-permute-start = (f32[4,128,256]{2,1,0:T(8,128)}, f32[4,128,256]{2,1,0:T(8,128)S(1)}, u32[]{:S(2)}, u32[]{:S(2)}) collective-permute-start(f32[4,128,256]{2,1,0:T(8,128)} %convolution_add_fusion.5), channel_id=1, source_target_pairs={{0,4},{4,8},{8,12},{12,16},{16,20},{20,24},{24,28},{28,32},{32,36}... | collective-permute-start | bytes 1572872 | tf_op jit(solution)/shard_map/while/body/eval_jaxpr/ppermute | solution.py:15
  464.6 12.8 %collective-permute-start = (f32[4,128,256]{2,1,0:T(8,128)}, f32[4,128,256]{2,1,0:T(8,128)S(1)}, u32[]{:S(2)}, u32[]{:S(2)}) collective-permute-start(f32[4,128,256]{2,1,0:T(8,128)} %convolution_add_fusion.5), channel_id=1, source_target_pairs={{0,4},{4,8},{8,12},{12,16},{16,20},{20,24},{24,28},{28,32},{32,36}... | collective-permute-start | bytes 1572872 | tf_op jit(solution)/shard_map/while/body/eval_jaxpr/ppermute | solution.py:15
  479.7 12.8 %collective-permute-start = (f32[4,128,256]{2,1,0:T(8,128)}, f32[4,128,256]{2,1,0:T(8,128)S(1)}, u32[]{:S(2)}, u32[]{:S(2)}) collective-permute-start(f32[4,128,256]{2,1,0:T(8,128)} %convolution_add_fusion.5), channel_id=1, source_target_pairs={{0,4},{4,8},{8,12},{12,16},{16,20},{20,24},{24,28},{28,32},{32,36}... | collective-permute-start | bytes 1572872 | tf_op jit(solution)/shard_map/while/body/eval_jaxpr/ppermute | solution.py:15
  494.9 12.8 %collective-permute-start = (f32[4,128,256]{2,1,0:T(8,128)}, f32[4,128,256]{2,1,0:T(8,128)S(1)}, u32[]{:S(2)}, u32[]{:S(2)}) collective-permute-start(f32[4,128,256]{2,1,0:T(8,128)} %convolution_add_fusion.5), channel_id=1, source_target_pairs={{0,4},{4,8},{8,12},{12,16},{16,20},{20,24},{24,28},{28,32},{32,36}... | collective-permute-start | bytes 1572872 | tf_op jit(solution)/shard_map/while/body/eval_jaxpr/ppermute | solution.py:15
  510.0 12.8 %collective-permute-start = (f32[4,128,256]{2,1,0:T(8,128)}, f32[4,128,256]{2,1,0:T(8,128)S(1)}, u32[]{:S(2)}, u32[]{:S(2)}) collective-permute-start(f32[4,128,256]{2,1,0:T(8,128)} %convolution_add_fusion.5), channel_id=1, source_target_pairs={{0,4},{4,8},{8,12},{12,16},{16,20},{20,24},{24,28},{28,32},{32,36}... | collective-permute-start | bytes 1572872 | tf_op jit(solution)/shard_map/while/body/eval_jaxpr/ppermute | solution.py:15
  525.1 12.8 %collective-permute-start = (f32[4,128,256]{2,1,0:T(8,128)}, f32[4,128,256]{2,1,0:T(8,128)S(1)}, u32[]{:S(2)}, u32[]{:S(2)}) collective-permute-start(f32[4,128,256]{2,1,0:T(8,128)} %convolution_add_fusion.5), channel_id=1, source_target_pairs={{0,4},{4,8},{8,12},{12,16},{16,20},{20,24},{24,28},{28,32},{32,36}... | collective-permute-start | bytes 1572872 | tf_op jit(solution)/shard_map/while/body/eval_jaxpr/ppermute | solution.py:15
  540.3 12.8 %collective-permute-start = (f32[4,128,256]{2,1,0:T(8,128)}, f32[4,128,256]{2,1,0:T(8,128)S(1)}, u32[]{:S(2)}, u32[]{:S(2)}) collective-permute-start(f32[4,128,256]{2,1,0:T(8,128)} %convolution_add_fusion.5), channel_id=1, source_target_pairs={{0,4},{4,8},{8,12},{12,16},{16,20},{20,24},{24,28},{28,32},{32,36}... | collective-permute-start | bytes 1572872 | tf_op jit(solution)/shard_map/while/body/eval_jaxpr/ppermute | solution.py:15
  555.4 12.8 %collective-permute-start = (f32[4,128,256]{2,1,0:T(8,128)}, f32[4,128,256]{2,1,0:T(8,128)S(1)}, u32[]{:S(2)}, u32[]{:S(2)}) collective-permute-start(f32[4,128,256]{2,1,0:T(8,128)} %convolution_add_fusion.5), channel_id=1, source_target_pairs={{0,4},{4,8},{8,12},{12,16},{16,20},{20,24},{24,28},{28,32},{32,36}... | collective-permute-start | bytes 1572872 | tf_op jit(solution)/shard_map/while/body/eval_jaxpr/ppermute | solution.py:15
  570.5 12.8 %collective-permute-start = (f32[4,128,256]{2,1,0:T(8,128)}, f32[4,128,256]{2,1,0:T(8,128)S(1)}, u32[]{:S(2)}, u32[]{:S(2)}) collective-permute-start(f32[4,128,256]{2,1,0:T(8,128)} %convolution_add_fusion.5), channel_id=1, source_target_pairs={{0,4},{4,8},{8,12},{12,16},{16,20},{20,24},{24,28},{28,32},{32,36}... | collective-permute-start | bytes 1572872 | tf_op jit(solution)/shard_map/while/body/eval_jaxpr/ppermute | solution.py:15
  585.7 12.8 %collective-permute-start = (f32[4,128,256]{2,1,0:T(8,128)}, f32[4,128,256]{2,1,0:T(8,128)S(1)}, u32[]{:S(2)}, u32[]{:S(2)}) collective-permute-start(f32[4,128,256]{2,1,0:T(8,128)} %convolution_add_fusion.5), channel_id=1, source_target_pairs={{0,4},{4,8},{8,12},{12,16},{16,20},{20,24},{24,28},{28,32},{32,36}... | collective-permute-start | bytes 1572872 | tf_op jit(solution)/shard_map/while/body/eval_jaxpr/ppermute | solution.py:15
  600.8 12.8 %collective-permute-start = (f32[4,128,256]{2,1,0:T(8,128)}, f32[4,128,256]{2,1,0:T(8,128)S(1)}, u32[]{:S(2)}, u32[]{:S(2)}) collective-permute-start(f32[4,128,256]{2,1,0:T(8,128)} %convolution_add_fusion.5), channel_id=1, source_target_pairs={{0,4},{4,8},{8,12},{12,16},{16,20},{20,24},{24,28},{28,32},{32,36}... | collective-permute-start | bytes 1572872 | tf_op jit(solution)/shard_map/while/body/eval_jaxpr/ppermute | solution.py:15
  (49 other events, 547.6 us)
Sparse Core Ops, SparseCore 0:
  629.0 97.7 all-reduce.3
where the time goes:
time: 935 us; the launch traced here: 932 us
  waiting for transfers between devices  288 us (31%)
  blocking collectives  190 us (20%)
  starting transfers between devices  161 us (17%)
  matrix products  136 us (15%)
  other arithmetic  100 us (11%)
  local copies, waits for them, and re-layouts  40.7 us (4%)
  between operations  14.5 us (2%)
    ppermute x32, waiting for transfers between devices, from_behind(): lax.ppermute(value, axis, [(source, source + steps) for source in range(f...  199 us
    ppermute x32, starting transfers between devices, from_behind(): lax.ppermute(value, axis, [(source, source + steps) for source in range(f...  161 us
    psum x1, blocking collectives, body(): last_rows = lax.psum(picked.astype(jnp.bfloat16), 'seq').astype(jnp.float32)  123 us
    psum x1, waiting for transfers between devices, body(): summed = lax.psum(partial_out, 'tp')  89.2 us
    another operation x12, other arithmetic, block_step(): lax.linalg.triangular_solve(system_mat, right_side, left_side=True, lower...  81.6 us
    dot_general x31, matrix products, relay_turn(): jnp.einsum('hde,hef->hdf', lin_map, incoming, precision=HIGH) + offset_state  72.1 us
    pmax x1, blocking collectives, body(): max_logit = lax.pmax(jnp.max(logits, axis=1), ('seq', 'tp'))  67.2 us
  transfers between devices with their start and end apart: 33, of which 32 were waited for; matrix products, arithmetic and copies ran while one was open for 2% of the time, Pallas kernels for 0%

commit v1 on v0

--- a/solution.py
+++ b/solution.py
@@ -172,7 +172,7 @@
     col_start = lax.axis_index("tp") * share_cols
     last_tok = ends * BLOCK_LEN - 1
     picker = (last_tok[:, None] == positions[None, :]).astype(jnp.bfloat16)
-    summed = lax.psum(partial_out, "tp")
+    summed = jnp.sum(lax.all_gather(partial_out, "tp"), axis=0)
     hidden_full = (x_float + summed).astype(jnp.bfloat16)
     hidden = lax.dynamic_slice_in_dim(hidden_full, col_start, share_cols, 1)
     picked = jnp.dot(picker, hidden_full, preferred_element_type=jnp.float32)

time: 935 us -> 868 us (0.928)
  matrix products: 136 us -> 76.1 us
  local copies, waits for them, and re-layouts: 40.7 us -> 21.4 us
  waiting for transfers between devices: 288 us -> 303 us
    all_gather x0 -> x1, waiting for transfers between devices: none -> 114 us  [body(): summed = jnp.sum(lax.all_gather(partial_out, 'tp'), axis=0)]
    psum x1 -> x0, waiting for transfers between devices: 89.2 us -> none  [body(): summed = lax.psum(partial_out, 'tp')]
    dot_general x31, matrix products: 72.1 us -> 18.1 us  [relay_turn(): jnp.einsum('hde,hef->hdf', lin_map, incoming, precision=HIGH) + offset_state]
    ppermute x32, waiting for transfers between devices: 199 us -> 189 us  [from_behind(): lax.ppermute(value, axis, [(source, source + steps) for source in range(f...]
  transfers between devices with their start and end apart: 33 -> 33, of which waited for: 32 -> 32; matrix products, arithmetic and copies ran while one was open for 2% -> 1% of each run, Pallas kernels for 0% -> 0%
where the time goes in v1:
time: 868 us; the launch traced here: 867 us
  waiting for transfers between devices  303 us (35%)
  blocking collectives  190 us (22%)
  starting transfers between devices  167 us (19%)
  other arithmetic  93.4 us (11%)
  matrix products  76.1 us (9%)
  local copies, waits for them, and re-layouts  21.4 us (2%)
  between operations  14.6 us (2%)
    ppermute x32, waiting for transfers between devices, from_behind(): lax.ppermute(value, axis, [(source, source + steps) for source in range(f...  189 us
    ppermute x32, starting transfers between devices, from_behind(): lax.ppermute(value, axis, [(source, source + steps) for source in range(f...  167 us
    psum x1, blocking collectives, body(): last_rows = lax.psum(picked.astype(jnp.bfloat16), 'seq').astype(jnp.float32)  123 us
    all_gather x1, waiting for transfers between devices, body(): summed = jnp.sum(lax.all_gather(partial_out, 'tp'), axis=0)  114 us
    another operation x12, other arithmetic, block_step(): lax.linalg.triangular_solve(system_mat, right_side, left_side=True, lower...  78.7 us
    pmax x1, blocking collectives, body(): max_logit = lax.pmax(jnp.max(logits, axis=1), ('seq', 'tp'))  67.1 us
    dot_general x31, matrix products, relay_turn(): jnp.einsum('hde,hef->hdf', lin_map, incoming, precision=HIGH) + offset_state  18.1 us
  transfers between devices with their start and end apart: 33, of which 32 were waited for; matrix products, arithmetic and copies ran while one was open for 1% of the time, Pallas kernels for 0%

profile of v1, /device:TPU:1, one launch (start us, length us, event | category | flops | bytes accessed | tf_op | source)
XLA Modules:
  0.0 866.9 jit_solution(3189869595160729459)
XLA Ops:
  33.9 117.3 %while.24 = (s32[]{:T(128)}, f32[4,128,384]{2,1,0:T(8,128)S(1)}, f32[4,4,64,384]{3,2,0,1:T(8,128)}, f32[4,4,128,384]{3,2,1,0:T(8,128)}, f32[4,4,64]{2,1,0:T(4,12...) while((s32[]{:T(128)}, f32[4,128,384]{2,1,0:T(8,128)S(1)}, ...), condition=%wide.region_8.9_spmd, body=%wide.region_7.8_spmd.sunk | while | flops 656073024 | bytes 8813277 | solution.py:145
  34.4 19.7 %custom-call.8 = f32[4,1,64,64]{2,3,1,0:T(8,128)S(1)} custom-call(f32[4,1,64,64]{3,2,1,0:T(8,128)S(1)} %fusion.136), custom_call_target="InvertDiagBlocksLowerTriangular" | custom-call | tf_op jit(solution)/shard_map/while/body/eval_jaxpr/triangular_solve | solution.py:62
  63.8 19.7 %custom-call.8 = f32[4,1,64,64]{2,3,1,0:T(8,128)S(1)} custom-call(f32[4,1,64,64]{3,2,1,0:T(8,128)S(1)} %fusion.136), custom_call_target="InvertDiagBlocksLowerTriangular" | custom-call | tf_op jit(solution)/shard_map/while/body/eval_jaxpr/triangular_solve | solution.py:62
  93.1 19.7 %custom-call.8 = f32[4,1,64,64]{2,3,1,0:T(8,128)S(1)} custom-call(f32[4,1,64,64]{3,2,1,0:T(8,128)S(1)} %fusion.136), custom_call_target="InvertDiagBlocksLowerTriangular" | custom-call | tf_op jit(solution)/shard_map/while/body/eval_jaxpr/triangular_solve | solution.py:62
  122.4 19.7 %custom-call.8 = f32[4,1,64,64]{2,3,1,0:T(8,128)S(1)} custom-call(f32[4,1,64,64]{3,2,1,0:T(8,128)S(1)} %fusion.136), custom_call_target="InvertDiagBlocksLowerTriangular" | custom-call | tf_op jit(solution)/shard_map/while/body/eval_jaxpr/triangular_solve | solution.py:62
  151.3 369.9 %while.25 = (s32[]{:T(128)}, f32[4,128,256]{2,1,0:T(8,128)S(1)}, f32[4,128,128]{2,1,0:T(8,128)S(1)}, f32[4,128,256]{2,1,0:T(8,128)S(1)}, s32[]{:T(128)}) while((s32[]{:T(128)}, f32[4,128,256]{2,1,0:T(8,128)S(1)}, f32[4,128,128]{2,1,0:T(8,128)S(1)}, f32[4,128,256]{2,1,0:T(8,128)S(1)}, s32[]{:T(128)}) %tuple.76), condition=%wide.region_10.11_spmd, body=%wide.region_9.10_spmd.sunk | while | flops 201457664 | bytes 3932261 | solution.py:155
  153.9 6.1 collective-permute-done
  350.2 6.5 collective-permute-start
  363.4 6.5 collective-permute-start
  376.6 6.5 collective-permute-start
  389.8 6.5 collective-permute-start
  403.0 6.5 collective-permute-start
  416.2 6.5 collective-permute-start
  429.4 6.5 collective-permute-start
  442.6 6.5 collective-permute-start
  455.8 6.5 collective-permute-start
  469.0 6.5 collective-permute-start
  482.2 6.5 collective-permute-start
  495.4 6.5 collective-permute-start
  508.6 6.5 collective-permute-start
  527.6 7.6 fusion.47
  544.1 113.9 %all-gather.3.cloned.1.call-done = f32[1024,2048]{1,0:T(8,128)} async-done(((f32[256,2048]{1,0:T(8,128)}), f32[1024,2048]{1,0:T(8,128)}) %all-gather.3.cloned.1.call-update) | async-done | bytes 8388624 | tf_op jit(solution)/shard_map/all_gather | solution.py:175
  664.2 123.1 %psum.7 = bf16[4,2048]{1,0:T(4,128)(2,1)S(1)} all-reduce(bf16[4,2048]{1,0:T(4,128)(2,1)S(1)} %convolution_convert_fusion), channel_id=1, replica_groups=mesh['seq'=32,'tp'=4] {'seq'}, use_global_device_ids=true, to_apply=%region_13.14 | all-reduce | flops 8192 | bytes 32768 | tf_op jit(solution)/shard_map/psum | solution.py:179
  792.1 67.1 %pmax.7 = f32[4]{0:T(128)} all-reduce(f32[4]{0:T(128)S(1)} %convolution_reduce_fusion), channel_id=1, replica_groups=mesh['seq'=32,'tp'=4] {'seq','tp'}, use_global_device_ids=true, to_apply=%region_16.17 | all-reduce | flops 4 | bytes 32 | tf_op jit(solution)/shard_map/pmax | solution.py:182
  (266 shorter events, 370.3 us)
Async XLA Ops:
  7.2 650.8 %all-gather.3.cloned.1.call-start = ((), (), s32[]{:S(2)}) async-start(), calls=%async_computation | async-start | bytes 10485760 | tf_op jit(solution)/shard_map/all_gather | solution.py:175
  193.8 10.5 %collective-permute-start = (f32[4,128,256]{2,1,0:T(8,128)S(1)}, f32[4,128,256]{2,1,0:T(8,128)S(1)}, u32[]{:S(2)}, u32[]{:S(2)}) collective-permute-start(f32[4,128,256]{2,1,0:T(8,128)S(1)} %convolution_add_fusion.5), channel_id=1, source_target_pairs={{0,4},{4,8},{8,12},{12,16},{16,20},{20,24},{24,28},{28,32},{32,36}... | collective-permute-start | bytes 1572872 | tf_op jit(solution)/shard_map/while/body/eval_jaxpr/ppermute | solution.py:15
  204.9 10.5 %collective-permute-start = (f32[4,128,256]{2,1,0:T(8,128)S(1)}, f32[4,128,256]{2,1,0:T(8,128)S(1)}, u32[]{:S(2)}, u32[]{:S(2)}) collective-permute-start(f32[4,128,256]{2,1,0:T(8,128)S(1)} %convolution_add_fusion.5), channel_id=1, source_target_pairs={{0,4},{4,8},{8,12},{12,16},{16,20},{20,24},{24,28},{28,32},{32,36}... | collective-permute-start | bytes 1572872 | tf_op jit(solution)/shard_map/while/body/eval_jaxpr/ppermute | solution.py:15
  216.0 10.5 %collective-permute-start = (f32[4,128,256]{2,1,0:T(8,128)S(1)}, f32[4,128,256]{2,1,0:T(8,128)S(1)}, u32[]{:S(2)}, u32[]{:S(2)}) collective-permute-start(f32[4,128,256]{2,1,0:T(8,128)S(1)} %convolution_add_fusion.5), channel_id=1, source_target_pairs={{0,4},{4,8},{8,12},{12,16},{16,20},{20,24},{24,28},{28,32},{32,36}... | collective-permute-start | bytes 1572872 | tf_op jit(solution)/shard_map/while/body/eval_jaxpr/ppermute | solution.py:15
  238.2 10.5 %collective-permute-start = (f32[4,128,256]{2,1,0:T(8,128)S(1)}, f32[4,128,256]{2,1,0:T(8,128)S(1)}, u32[]{:S(2)}, u32[]{:S(2)}) collective-permute-start(f32[4,128,256]{2,1,0:T(8,128)S(1)} %convolution_add_fusion.5), channel_id=1, source_target_pairs={{0,4},{4,8},{8,12},{12,16},{16,20},{20,24},{24,28},{28,32},{32,36}... | collective-permute-start | bytes 1572872 | tf_op jit(solution)/shard_map/while/body/eval_jaxpr/ppermute | solution.py:15
  249.3 10.5 %collective-permute-start = (f32[4,128,256]{2,1,0:T(8,128)S(1)}, f32[4,128,256]{2,1,0:T(8,128)S(1)}, u32[]{:S(2)}, u32[]{:S(2)}) collective-permute-start(f32[4,128,256]{2,1,0:T(8,128)S(1)} %convolution_add_fusion.5), channel_id=1, source_target_pairs={{0,4},{4,8},{8,12},{12,16},{16,20},{20,24},{24,28},{28,32},{32,36}... | collective-permute-start | bytes 1572872 | tf_op jit(solution)/shard_map/while/body/eval_jaxpr/ppermute | solution.py:15
  260.4 10.5 %collective-permute-start = (f32[4,128,256]{2,1,0:T(8,128)S(1)}, f32[4,128,256]{2,1,0:T(8,128)S(1)}, u32[]{:S(2)}, u32[]{:S(2)}) collective-permute-start(f32[4,128,256]{2,1,0:T(8,128)S(1)} %convolution_add_fusion.5), channel_id=1, source_target_pairs={{0,4},{4,8},{8,12},{12,16},{16,20},{20,24},{24,28},{28,32},{32,36}... | collective-permute-start | bytes 1572872 | tf_op jit(solution)/shard_map/while/body/eval_jaxpr/ppermute | solution.py:15
  271.5 10.5 %collective-permute-start = (f32[4,128,256]{2,1,0:T(8,128)S(1)}, f32[4,128,256]{2,1,0:T(8,128)S(1)}, u32[]{:S(2)}, u32[]{:S(2)}) collective-permute-start(f32[4,128,256]{2,1,0:T(8,128)S(1)} %convolution_add_fusion.5), channel_id=1, source_target_pairs={{0,4},{4,8},{8,12},{12,16},{16,20},{20,24},{24,28},{28,32},{32,36}... | collective-permute-start | bytes 1572872 | tf_op jit(solution)/shard_map/while/body/eval_jaxpr/ppermute | solution.py:15
  315.9 10.5 %collective-permute-start = (f32[4,128,256]{2,1,0:T(8,128)S(1)}, f32[4,128,256]{2,1,0:T(8,128)S(1)}, u32[]{:S(2)}, u32[]{:S(2)}) collective-permute-start(f32[4,128,256]{2,1,0:T(8,128)S(1)} %convolution_add_fusion.5), channel_id=1, source_target_pairs={{0,4},{4,8},{8,12},{12,16},{16,20},{20,24},{24,28},{28,32},{32,36}... | collective-permute-start | bytes 1572872 | tf_op jit(solution)/shard_map/while/body/eval_jaxpr/ppermute | solution.py:15
  327.0 10.5 %collective-permute-start = (f32[4,128,256]{2,1,0:T(8,128)S(1)}, f32[4,128,256]{2,1,0:T(8,128)S(1)}, u32[]{:S(2)}, u32[]{:S(2)}) collective-permute-start(f32[4,128,256]{2,1,0:T(8,128)S(1)} %convolution_add_fusion.5), channel_id=1, source_target_pairs={{0,4},{4,8},{8,12},{12,16},{16,20},{20,24},{24,28},{28,32},{32,36}... | collective-permute-start | bytes 1572872 | tf_op jit(solution)/shard_map/while/body/eval_jaxpr/ppermute | solution.py:15
  338.1 11.5 %collective-permute-start = (f32[4,128,256]{2,1,0:T(8,128)S(1)}, f32[4,128,256]{2,1,0:T(8,128)S(1)}, u32[]{:S(2)}, u32[]{:S(2)}) collective-permute-start(f32[4,128,256]{2,1,0:T(8,128)S(1)} %convolution_add_fusion.5), channel_id=1, source_target_pairs={{0,4},{4,8},{8,12},{12,16},{16,20},{20,24},{24,28},{28,32},{32,36}... | collective-permute-start | bytes 1572872 | tf_op jit(solution)/shard_map/while/body/eval_jaxpr/ppermute | solution.py:15
  350.2 12.6 %collective-permute-start = (f32[4,128,256]{2,1,0:T(8,128)S(1)}, f32[4,128,256]{2,1,0:T(8,128)S(1)}, u32[]{:S(2)}, u32[]{:S(2)}) collective-permute-start(f32[4,128,256]{2,1,0:T(8,128)S(1)} %convolution_add_fusion.5), channel_id=1, source_target_pairs={{0,4},{4,8},{8,12},{12,16},{16,20},{20,24},{24,28},{28,32},{32,36}... | collective-permute-start | bytes 1572872 | tf_op jit(solution)/shard_map/while/body/eval_jaxpr/ppermute | solution.py:15
  363.4 12.6 %collective-permute-start = (f32[4,128,256]{2,1,0:T(8,128)S(1)}, f32[4,128,256]{2,1,0:T(8,128)S(1)}, u32[]{:S(2)}, u32[]{:S(2)}) collective-permute-start(f32[4,128,256]{2,1,0:T(8,128)S(1)} %convolution_add_fusion.5), channel_id=1, source_target_pairs={{0,4},{4,8},{8,12},{12,16},{16,20},{20,24},{24,28},{28,32},{32,36}... | collective-permute-start | bytes 1572872 | tf_op jit(solution)/shard_map/while/body/eval_jaxpr/ppermute | solution.py:15
  376.6 12.6 %collective-permute-start = (f32[4,128,256]{2,1,0:T(8,128)S(1)}, f32[4,128,256]{2,1,0:T(8,128)S(1)}, u32[]{:S(2)}, u32[]{:S(2)}) collective-permute-start(f32[4,128,256]{2,1,0:T(8,128)S(1)} %convolution_add_fusion.5), channel_id=1, source_target_pairs={{0,4},{4,8},{8,12},{12,16},{16,20},{20,24},{24,28},{28,32},{32,36}... | collective-permute-start | bytes 1572872 | tf_op jit(solution)/shard_map/while/body/eval_jaxpr/ppermute | solution.py:15
  389.8 12.6 %collective-permute-start = (f32[4,128,256]{2,1,0:T(8,128)S(1)}, f32[4,128,256]{2,1,0:T(8,128)S(1)}, u32[]{:S(2)}, u32[]{:S(2)}) collective-permute-start(f32[4,128,256]{2,1,0:T(8,128)S(1)} %convolution_add_fusion.5), channel_id=1, source_target_pairs={{0,4},{4,8},{8,12},{12,16},{16,20},{20,24},{24,28},{28,32},{32,36}... | collective-permute-start | bytes 1572872 | tf_op jit(solution)/shard_map/while/body/eval_jaxpr/ppermute | solution.py:15
  403.0 12.6 %collective-permute-start = (f32[4,128,256]{2,1,0:T(8,128)S(1)}, f32[4,128,256]{2,1,0:T(8,128)S(1)}, u32[]{:S(2)}, u32[]{:S(2)}) collective-permute-start(f32[4,128,256]{2,1,0:T(8,128)S(1)} %convolution_add_fusion.5), channel_id=1, source_target_pairs={{0,4},{4,8},{8,12},{12,16},{16,20},{20,24},{24,28},{28,32},{32,36}... | collective-permute-start | bytes 1572872 | tf_op jit(solution)/shard_map/while/body/eval_jaxpr/ppermute | solution.py:15
  416.2 12.6 %collective-permute-start = (f32[4,128,256]{2,1,0:T(8,128)S(1)}, f32[4,128,256]{2,1,0:T(8,128)S(1)}, u32[]{:S(2)}, u32[]{:S(2)}) collective-permute-start(f32[4,128,256]{2,1,0:T(8,128)S(1)} %convolution_add_fusion.5), channel_id=1, source_target_pairs={{0,4},{4,8},{8,12},{12,16},{16,20},{20,24},{24,28},{28,32},{32,36}... | collective-permute-start | bytes 1572872 | tf_op jit(solution)/shard_map/while/body/eval_jaxpr/ppermute | solution.py:15
  429.4 12.6 %collective-permute-start = (f32[4,128,256]{2,1,0:T(8,128)S(1)}, f32[4,128,256]{2,1,0:T(8,128)S(1)}, u32[]{:S(2)}, u32[]{:S(2)}) collective-permute-start(f32[4,128,256]{2,1,0:T(8,128)S(1)} %convolution_add_fusion.5), channel_id=1, source_target_pairs={{0,4},{4,8},{8,12},{12,16},{16,20},{20,24},{24,28},{28,32},{32,36}... | collective-permute-start | bytes 1572872 | tf_op jit(solution)/shard_map/while/body/eval_jaxpr/ppermute | solution.py:15
  442.6 12.6 %collective-permute-start = (f32[4,128,256]{2,1,0:T(8,128)S(1)}, f32[4,128,256]{2,1,0:T(8,128)S(1)}, u32[]{:S(2)}, u32[]{:S(2)}) collective-permute-start(f32[4,128,256]{2,1,0:T(8,128)S(1)} %convolution_add_fusion.5), channel_id=1, source_target_pairs={{0,4},{4,8},{8,12},{12,16},{16,20},{20,24},{24,28},{28,32},{32,36}... | collective-permute-start | bytes 1572872 | tf_op jit(solution)/shard_map/while/body/eval_jaxpr/ppermute | solution.py:15
  455.8 12.6 %collective-permute-start = (f32[4,128,256]{2,1,0:T(8,128)S(1)}, f32[4,128,256]{2,1,0:T(8,128)S(1)}, u32[]{:S(2)}, u32[]{:S(2)}) collective-permute-start(f32[4,128,256]{2,1,0:T(8,128)S(1)} %convolution_add_fusion.5), channel_id=1, source_target_pairs={{0,4},{4,8},{8,12},{12,16},{16,20},{20,24},{24,28},{28,32},{32,36}... | collective-permute-start | bytes 1572872 | tf_op jit(solution)/shard_map/while/body/eval_jaxpr/ppermute | solution.py:15
  469.0 12.6 %collective-permute-start = (f32[4,128,256]{2,1,0:T(8,128)S(1)}, f32[4,128,256]{2,1,0:T(8,128)S(1)}, u32[]{:S(2)}, u32[]{:S(2)}) collective-permute-start(f32[4,128,256]{2,1,0:T(8,128)S(1)} %convolution_add_fusion.5), channel_id=1, source_target_pairs={{0,4},{4,8},{8,12},{12,16},{16,20},{20,24},{24,28},{28,32},{32,36}... | collective-permute-start | bytes 1572872 | tf_op jit(solution)/shard_map/while/body/eval_jaxpr/ppermute | solution.py:15
  482.2 12.6 %collective-permute-start = (f32[4,128,256]{2,1,0:T(8,128)S(1)}, f32[4,128,256]{2,1,0:T(8,128)S(1)}, u32[]{:S(2)}, u32[]{:S(2)}) collective-permute-start(f32[4,128,256]{2,1,0:T(8,128)S(1)} %convolution_add_fusion.5), channel_id=1, source_target_pairs={{0,4},{4,8},{8,12},{12,16},{16,20},{20,24},{24,28},{28,32},{32,36}... | collective-permute-start | bytes 1572872 | tf_op jit(solution)/shard_map/while/body/eval_jaxpr/ppermute | solution.py:15
  495.4 12.6 %collective-permute-start = (f32[4,128,256]{2,1,0:T(8,128)S(1)}, f32[4,128,256]{2,1,0:T(8,128)S(1)}, u32[]{:S(2)}, u32[]{:S(2)}) collective-permute-start(f32[4,128,256]{2,1,0:T(8,128)S(1)} %convolution_add_fusion.5), channel_id=1, source_target_pairs={{0,4},{4,8},{8,12},{12,16},{16,20},{20,24},{24,28},{28,32},{32,36}... | collective-permute-start | bytes 1572872 | tf_op jit(solution)/shard_map/while/body/eval_jaxpr/ppermute | solution.py:15
  508.6 12.6 %collective-permute-start = (f32[4,128,256]{2,1,0:T(8,128)S(1)}, f32[4,128,256]{2,1,0:T(8,128)S(1)}, u32[]{:S(2)}, u32[]{:S(2)}) collective-permute-start(f32[4,128,256]{2,1,0:T(8,128)S(1)} %convolution_add_fusion.5), channel_id=1, source_target_pairs={{0,4},{4,8},{8,12},{12,16},{16,20},{20,24},{24,28},{28,32},{32,36}... | collective-permute-start | bytes 1572872 | tf_op jit(solution)/shard_map/while/body/eval_jaxpr/ppermute | solution.py:15
  (31 other events, 371.2 us)
Sparse Core Ops, SparseCore 0:
  535.4 122.5 all-gather.2
